TPU v7x, 32 devices: a whole 2x2x4 slice. The times are simulated.
32 devices in a mesh: row: 4 (over y, x), col: 8 (over z, core).
Axes of the slice: x: 2, y: 2, z: 4, core: 2. Of those that a mesh axis runs over, the one named last changes fastest.
Arguments:
- points: bfloat16 [8192, 256], P(('row', 'col')), may hold values from -0.4 to 0.4, as said below
- spread: float32 [8192], P(('row', 'col')), may hold values from 1 to 12
- vectors: bfloat16 [8192, 64], P(('row', 'col')), may hold values from -6 to 6
Outputs:
- product: float32 [8192, 64], P(('row', 'col'))
Inputs may be any that keep to these rules, and one draw needn't show every extreme that they name: `points`: embedding entries are real values of order 0.1.
All inputs are finite; a program needn't handle non-finite values.
Results may differ from a plain program's by a relative error of at most 0.0085.
Values may be sent and summed in bfloat16 or wider, within the bound.
A program may use at most 128 MiB of HBM per device.

v0:
```python
import jax
import jax.numpy as jnp
from jax import lax
from jax.sharding import PartitionSpec as P


def distances(left_pts, right_pts):
    left_f = left_pts.astype(jnp.float32)
    right_f = right_pts.astype(jnp.float32)
    left_sq = jnp.sum(left_f * left_f, axis=1)
    right_sq = jnp.sum(right_f * right_f, axis=1)
    cross = lax.dot_general(
        left_pts, right_pts, (((1,), (1,)), ((), ())), preferred_element_type=jnp.float32
    )
    return left_sq[:, None] + right_sq[None, :] - 2.0 * cross


def local(points, spread, vectors):
    share_rows = points.shape[0]
    n_rows = lax.axis_size("row")
    n_cols = lax.axis_size("col")
    row_pos = lax.axis_index("row")
    col_pos = lax.axis_index("col")
    blk_pts, blk_bw, blk_vec = (
        lax.all_gather(points, "col", axis=0, tiled=True),
        lax.all_gather(spread.astype(jnp.bfloat16), "col", axis=0, tiled=True).astype(spread.dtype),
        lax.all_gather(vectors, "col", axis=0, tiled=True),
    )
    crs_pts, crs_bw, crs_vec = (
        lax.all_gather(points, "row", axis=0, tiled=True),
        lax.all_gather(spread.astype(jnp.bfloat16), "row", axis=0, tiled=True).astype(spread.dtype),
        lax.all_gather(vectors, "row", axis=0, tiled=True),
    )
    blk_local = jnp.arange(share_rows * n_cols, dtype=jnp.int32)
    blk_ids = row_pos * (n_cols * share_rows) + blk_local
    crs_local = jnp.arange(share_rows * n_rows, dtype=jnp.int32)
    crs_ids = (
        crs_local // share_rows * (n_cols * share_rows)
        + col_pos * share_rows
        + crs_local % share_rows
    )
    same = blk_ids[:, None] == crs_ids[None, :]
    dist = distances(blk_pts, crs_pts)
    kernel = jnp.where(same, jnp.float32(0.0), jnp.exp(-blk_bw[:, None] * dist))
    totals = lax.psum(jnp.sum(kernel, axis=1), "col")
    norm = (kernel / totals[:, None]).astype(jnp.bfloat16)
    to_cross = lax.dot_general(
        norm, blk_vec, (((0,), (0,)), ((), ())), preferred_element_type=jnp.float32
    )
    mirror = jnp.where(same, jnp.float32(0.0), jnp.exp(-crs_bw[None, :] * dist))
    mirror_tot = lax.psum(jnp.sum(mirror, axis=0), "row")
    mirror_norm = (mirror / mirror_tot[None, :]).astype(jnp.bfloat16)
    to_cross = to_cross + lax.dot_general(
        mirror_norm, blk_vec, (((0,), (0,)), ((), ())), preferred_element_type=jnp.float32
    )
    summed = lax.psum_scatter(to_cross, "row", scatter_dimension=0, tiled=True)
    return 0.5 * summed


def solution(mesh):
    placed = (P(("row", "col"), None), P(("row", "col")), P(("row", "col"), None))
    return jax.shard_map(
        local, mesh=mesh, in_specs=placed, out_specs=P(("row", "col"), None), check_vma=False
    )
```

profile of v0, /device:TPU:0, one launch (start us, length us, event | category | flops | bytes accessed | tf_op | source)
XLA Modules:
  0.0 126.9 jit_solution(6512187139585747209)
XLA Ops:
  6.5 0.0 all-gather.4.cloned.1.call-start
  6.5 0.7 all-gather.4.cloned.1.call-update
  7.3 0.0 reduce-scatter.2.cloned.1.call-start
  7.3 0.7 convert_element_type.22
  8.0 9.5 %all-gather.1 = bf16[4,1,256]{2,1,0:T(2,128)(2,1)S(1)} all-gather(bf16[1,1,256]{2,1,0:T(2,128)(2,1)S(1)} %reshape.35), channel_id=1, replica_groups=mesh['row'=4,'col'=8] {'row'}, dimensions={0}, use_global_device_ids=true | all-gather | bytes 2560 | tf_op jit(solution)/shard_map/all_gather | solution.py:31
  17.5 12.0 %all-gather = bf16[8,1,256]{2,1,0:T(2,128)(2,1)S(1)} all-gather(bf16[1,1,256]{2,1,0:T(2,128)(2,1)S(1)} %reshape.35), channel_id=1, replica_groups=mesh['row'=4,'col'=8] {'col'}, dimensions={0}, use_global_device_ids=true | all-gather | bytes 4608 | tf_op jit(solution)/shard_map/all_gather | solution.py:26
  29.5 10.3 %all_gather.17 = bf16[1024,256]{1,0:T(8,128)(2,1)S(1)} all-gather(bf16[256,256]{1,0:T(8,128)(2,1)} %param.3), channel_id=1, replica_groups=mesh['row'=4,'col'=8] {'row'}, dimensions={0}, use_global_device_ids=true | all-gather | bytes 655360 | tf_op jit(solution)/shard_map/all_gather | solution.py:30
  39.8 14.4 %all_gather.18 = bf16[2048,64]{0,1:T(8,128)(2,1)S(1)} all-gather(bf16[256,64]{0,1:T(8,128)(2,1)} %param.5), channel_id=1, replica_groups=mesh['row'=4,'col'=8] {'col'}, dimensions={0}, use_global_device_ids=true | all-gather | bytes 294912 | tf_op jit(solution)/shard_map/all_gather | solution.py:27
  54.2 0.2 multiply_reduce_fusion.1
  54.5 0.0 all-gather.4.cloned.1.call-done
  54.5 1.6 %multiply_reduce_fusion = f32[2048]{0:T(1024)S(1)} fusion(bf16[2048,256]{1,0:T(8,128)(2,1)} %all-gather.4.cloned.1.call-done), kind=kLoop, calls=%fused_computation.9 | loop fusion | flops 1570816 | bytes 1056768 | tf_op jit(solution)/shard_map/reduce_sum | solution.py:10
  56.1 7.5 %fusion = (f32[2048]{0:T(1024)S(1)}, f32[1024]{0:T(1024)S(1)}, f32[2048,1024]{1,0:T(8,128)}) fusion(f32[1024]{0:T(1024)S(1)} %multiply_reduce_fusion.1, f32[2048]{0:T(1024)S(1)} %multiply_reduce_fusion, f32[2048]{0:T(1024)S(1)} %bitcast.6, s32[1024]{0:T(1024)S(1)} %fusion.13, s32[2048]{0:T(1024)S(1)} %iota_add_fusion, f32[1024]{0:T(1024)S(1)} %bitcast.8, ...), kind=kOutput, calls=%fused_computation.5 | convolution fusion | flops 1094710272 | bytes 10010624 | tf_op jit(solution)/shard_map/dot_general | solution.py:12
  63.6 8.9 %psum.15 = f32[1024]{0:T(1024)S(1)} all-reduce(f32[1024]{0:T(1024)S(1)} %get-tuple-element.6), channel_id=1, replica_groups=mesh['row'=4,'col'=8] {'row'}, use_global_device_ids=true, to_apply=%region_5.6 | all-reduce | flops 1024 | bytes 8192 | tf_op jit(solution)/shard_map/psum | solution.py:51
  72.5 13.9 %psum.14 = f32[2048]{0:T(1024)S(1)} all-reduce(f32[2048]{0:T(1024)S(1)} %get-tuple-element.5), channel_id=1, replica_groups=mesh['row'=4,'col'=8] {'col'}, use_global_device_ids=true, to_apply=%region_3.4 | all-reduce | flops 2048 | bytes 16384 | tf_op jit(solution)/shard_map/psum | solution.py:45
  86.4 0.0 copy-start
  86.4 6.9 %fusion.2 = f32[1024,64]{0,1:T(8,128)S(1)} fusion(bf16[2048,64]{0,1:T(8,128)(2,1)S(1)} %all_gather.18, f32[2048,1024]{1,0:T(8,128)} %get-tuple-element.7, f32[1024]{0:T(1024)S(1)} %psum.15, f32[1024]{0:T(1024)S(1)} %bitcast.9, f32[1024]{0:T(1024)S(1)} %multiply_reduce_fusion.1, f32[2048]{0:T(1024)S(1)} %multiply_reduce_fusion, s32[1024]{0:T(1024)S(1)} %fusion.13, ...), kind=kOutput, calls=%fused_computation.7 | convolution fusion | flops 285212672 | bytes 8945664 | tf_op jit(solution)/shard_map/dot_general | solution.py:53
  93.3 0.0 copy-done
  93.3 3.8 %fusion.4 = f32[1024,64]{0,1:T(8,128)} fusion(f32[1024,64]{0,1:T(8,128)S(1)} %fusion.2, bf16[2048,64]{0,1:T(8,128)(2,1)S(1)} %all_gather.18, f32[2048,1024]{1,0:T(8,128)S(1)} %copy-done, f32[2048]{0:T(1024)S(1)} %psum.14, f32[1024]{0:T(1024)S(1)} %multiply_reduce_fusion.1, f32[2048]{0:T(1024)S(1)} %multiply_reduce_fusion, f32[2048]{0:T(1024)S(1)} %bitcast.7, ...), kind=kOutput, calls=%fused_computation.10 | convolution fusion | flops 285278208 | bytes 9216000 | tf_op jit(solution)/shard_map/dot_general | solution.py:47
  97.1 0.0 reduce-scatter.2.cloned.1.call-update
  97.2 21.5 %reduce-scatter.2.cloned.1.call-done = f32[256,64]{0,1:T(8,128)} async-done(((f32[1024,64]{0,1:T(8,128)}), f32[256,64]{0,1:T(8,128)}) %reduce-scatter.2.cloned.1.call-update) | async-done | bytes 65552 | tf_op jit(solution)/shard_map/reduce_scatter | solution.py:56
  118.6 1.5 %broadcast_multiply_fusion = f32[256,64]{0,1:T(8,128)} fusion(f32[256,64]{0,1:T(8,128)} %reduce-scatter.2.cloned.1.call-done), kind=kLoop, calls=%fused_computation.12 | loop fusion | flops 16384 | bytes 131072 | tf_op jit(solution)/shard_map/mul | solution.py:57
  (5 shorter events, 0.0 us)
Async XLA Ops:
  6.5 47.9 %all-gather.4.cloned.1.call-start = ((), (), s32[]{:S(2)}) async-start(), calls=%async_computation.1 | async-start | bytes 1179648 | tf_op jit(solution)/shard_map/all_gather | solution.py:25
  7.3 111.4 %reduce-scatter.2.cloned.1.call-start = ((), (), s32[]{:S(2)}) async-start(), calls=%async_computation.2 | async-start | bytes 327680 | tf_op jit(solution)/shard_map/reduce_scatter | solution.py:56
  86.4 6.9 %copy-start = (f32[2048,1024]{1,0:T(8,128)S(1)}, f32[2048,1024]{1,0:T(8,128)}, u32[]{:S(2)}) copy-start(f32[2048,1024]{1,0:T(8,128)} %get-tuple-element.7) | copy-start | bytes 25165828
Sparse Core Ops, SparseCore 0:
  9.0 24.7 all-gather.3
  97.3 21.3 reduce-scatter.1
where the time goes:
time: 127 us
  blocking collectives  69 us (54%)
  waiting for transfers between devices  22.2 us (17%)
  matrix products  18.2 us (14%)
  between operations  13.5 us (11%)
  other arithmetic  3.97 us (3%)
    reduce_scatter x1, waiting for transfers between devices, local(): summed = lax.psum_scatter(to_cross, 'row', scatter_dimension=0, tiled=True)  21.5 us
    all_gather x1, blocking collectives, local(): lax.all_gather(vectors, 'col', axis=0, tiled=True)  14.4 us
    psum x1, blocking collectives, local(): totals = lax.psum(jnp.sum(kernel, axis=1), 'col')  13.9 us
    all_gather x1, blocking collectives, local(): lax.all_gather(spread.astype(jnp.bfloat16), 'col', axis=0, tiled=True)  12 us
    all_gather x1, blocking collectives, local(): lax.all_gather(points, 'row', axis=0, tiled=True)  10.3 us
    all_gather x1, blocking collectives, local(): lax.all_gather(spread.astype(jnp.bfloat16), 'row', axis=0, tiled=True)  9.5 us
    psum x1, blocking collectives, local(): mirror_tot = lax.psum(jnp.sum(mirror, axis=0), 'row')  8.9 us
    dot_general x1, matrix products, distances(): lax.dot_general(left_pts, right_pts, (((1,), (1,)), ((), ())), preferred_...  7.5 us
  transfers between devices with their start and end apart: 2, of which 1 were waited for; matrix products, arithmetic and copies ran while one was open for 1% of the time, Pallas kernels for 0%

commit v1 on v0

--- a/solution.py
+++ b/solution.py
@@ -42,7 +42,7 @@
     same = blk_ids[:, None] == crs_ids[None, :]
     dist = distances(blk_pts, crs_pts)
     kernel = jnp.where(same, jnp.float32(0.0), jnp.exp(-blk_bw[:, None] * dist))
-    totals = lax.psum(jnp.sum(kernel, axis=1), "col")
+    totals = jnp.sum(lax.all_gather(jnp.sum(kernel, axis=1), "col"), axis=0)
     norm = (kernel / totals[:, None]).astype(jnp.bfloat16)
     to_cross = lax.dot_general(
         norm, blk_vec, (((0,), (0,)), ((), ())), preferred_element_type=jnp.float32

time: 127 us -> 127 us (level)
    all_gather x0 -> x1, blocking collectives: none -> 14 us  [local(): totals = jnp.sum(lax.all_gather(jnp.sum(kernel, axis=1), 'col'), axis=0)]
    psum x1 -> x0, blocking collectives: 13.9 us -> none  [local(): totals = lax.psum(jnp.sum(kernel, axis=1), 'col')]
where the time goes in v1:
time: 127 us
  blocking collectives  69.1 us (54%)
  waiting for transfers between devices  22.2 us (17%)
  matrix products  18.2 us (14%)
  between operations  13.5 us (11%)
  other arithmetic  3.99 us (3%)
    reduce_scatter x1, waiting for transfers between devices, local(): summed = lax.psum_scatter(to_cross, 'row', scatter_dimension=0, tiled=True)  21.5 us
    all_gather x1, blocking collectives, local(): lax.all_gather(vectors, 'col', axis=0, tiled=True)  14.4 us
    all_gather x1, blocking collectives, local(): totals = jnp.sum(lax.all_gather(jnp.sum(kernel, axis=1), 'col'), axis=0)  14 us
    all_gather x1, blocking collectives, local(): lax.all_gather(spread.astype(jnp.bfloat16), 'col', axis=0, tiled=True)  12 us
    all_gather x1, blocking collectives, local(): lax.all_gather(points, 'row', axis=0, tiled=True)  10.3 us
    all_gather x1, blocking collectives, local(): lax.all_gather(spread.astype(jnp.bfloat16), 'row', axis=0, tiled=True)  9.5 us
    psum x1, blocking collectives, local(): mirror_tot = lax.psum(jnp.sum(mirror, axis=0), 'row')  8.91 us
    dot_general x1, matrix products, distances(): lax.dot_general(left_pts, right_pts, (((1,), (1,)), ((), ())), preferred_...  7.49 us
  transfers between devices with their start and end apart: 2, of which 1 were waited for; matrix products, arithmetic and copies ran while one was open for 1% of the time, Pallas kernels for 0%

profile of v1, /device:TPU:0, one launch (start us, length us, event | category | flops | bytes accessed | tf_op | source)
XLA Modules:
  0.0 127.0 jit_solution(3339929738409985810)
XLA Ops:
  6.5 0.0 all-gather.5.cloned.1.call-start
  6.5 0.7 all-gather.5.cloned.1.call-update
  7.3 0.0 reduce-scatter.2.cloned.1.call-start
  7.3 0.7 convert_element_type.22
  8.0 9.5 %all-gather.2 = bf16[4,1,256]{2,1,0:T(2,128)(2,1)S(1)} all-gather(bf16[1,1,256]{2,1,0:T(2,128)(2,1)S(1)} %reshape.36), channel_id=1, replica_groups=mesh['row'=4,'col'=8] {'row'}, dimensions={0}, use_global_device_ids=true | all-gather | bytes 2560 | tf_op jit(solution)/shard_map/all_gather | solution.py:31
  17.5 12.0 %all-gather.1 = bf16[8,1,256]{2,1,0:T(2,128)(2,1)S(1)} all-gather(bf16[1,1,256]{2,1,0:T(2,128)(2,1)S(1)} %reshape.36), channel_id=1, replica_groups=mesh['row'=4,'col'=8] {'col'}, dimensions={0}, use_global_device_ids=true | all-gather | bytes 4608 | tf_op jit(solution)/shard_map/all_gather | solution.py:26
  29.5 10.3 %all_gather.23 = bf16[1024,256]{1,0:T(8,128)(2,1)S(1)} all-gather(bf16[256,256]{1,0:T(8,128)(2,1)} %param.3), channel_id=1, replica_groups=mesh['row'=4,'col'=8] {'row'}, dimensions={0}, use_global_device_ids=true | all-gather | bytes 655360 | tf_op jit(solution)/shard_map/all_gather | solution.py:30
  39.8 14.4 %all_gather.26 = bf16[2048,64]{0,1:T(8,128)(2,1)S(1)} all-gather(bf16[256,64]{0,1:T(8,128)(2,1)} %param.5), channel_id=1, replica_groups=mesh['row'=4,'col'=8] {'col'}, dimensions={0}, use_global_device_ids=true | all-gather | bytes 294912 | tf_op jit(solution)/shard_map/all_gather | solution.py:27
  54.2 0.2 multiply_reduce_fusion.1
  54.5 0.0 all-gather.5.cloned.1.call-done
  54.5 1.6 %multiply_reduce_fusion = f32[2048]{0:T(1024)S(1)} fusion(bf16[2048,256]{1,0:T(8,128)(2,1)} %all-gather.5.cloned.1.call-done), kind=kLoop, calls=%fused_computation.9 | loop fusion | flops 1570816 | bytes 1056768 | tf_op jit(solution)/shard_map/reduce_sum | solution.py:10
  56.1 7.5 %fusion = (f32[2048]{0:T(1024)S(1)}, f32[1024]{0:T(1024)S(1)}, f32[2048,1024]{1,0:T(8,128)}) fusion(f32[1024]{0:T(1024)S(1)} %multiply_reduce_fusion.1, f32[2048]{0:T(1024)S(1)} %multiply_reduce_fusion, f32[2048]{0:T(1024)S(1)} %bitcast.6, s32[1024]{0:T(1024)S(1)} %fusion.13, s32[2048]{0:T(1024)S(1)} %iota_add_fusion, f32[1024]{0:T(1024)S(1)} %bitcast.8, ...), kind=kOutput, calls=%fused_computation.5 | convolution fusion | flops 1094710272 | bytes 10010624 | tf_op jit(solution)/shard_map/dot_general | solution.py:12
  63.6 8.9 %psum.7 = f32[1024]{0:T(1024)S(1)} all-reduce(f32[1024]{0:T(1024)S(1)} %get-tuple-element.6), channel_id=1, replica_groups=mesh['row'=4,'col'=8] {'row'}, use_global_device_ids=true, to_apply=%region_5.6 | all-reduce | flops 1024 | bytes 8192 | tf_op jit(solution)/shard_map/psum | solution.py:51
  72.5 14.0 %all-gather = f32[16384]{0:T(1024)S(1)} all-gather(f32[2048]{0:T(1024)S(1)} %get-tuple-element.5), channel_id=2, replica_groups=mesh['row'=4,'col'=8] {'col'}, dimensions={0}, use_global_device_ids=true | all-gather | bytes 73728 | tf_op jit(solution)/shard_map/all_gather | solution.py:45
  86.5 0.0 copy-start
  86.5 6.9 %fusion.2 = f32[1024,64]{0,1:T(8,128)S(1)} fusion(bf16[2048,64]{0,1:T(8,128)(2,1)S(1)} %all_gather.26, f32[2048,1024]{1,0:T(8,128)} %get-tuple-element.7, f32[1024]{0:T(1024)S(1)} %psum.7, f32[1024]{0:T(1024)S(1)} %bitcast.9, f32[1024]{0:T(1024)S(1)} %multiply_reduce_fusion.1, f32[2048]{0:T(1024)S(1)} %multiply_reduce_fusion, s32[1024]{0:T(1024)S(1)} %fusion.13, ...), kind=kOutput, calls=%fused_computation.7 | convolution fusion | flops 285212672 | bytes 8945664 | tf_op jit(solution)/shard_map/dot_general | solution.py:53
  93.4 0.0 copy-done
  93.4 3.8 %fusion.4 = f32[1024,64]{0,1:T(8,128)} fusion(f32[1024,64]{0,1:T(8,128)S(1)} %fusion.2, bf16[2048,64]{0,1:T(8,128)(2,1)S(1)} %all_gather.26, f32[2048,1024]{1,0:T(8,128)S(1)} %copy-done, f32[2048]{0:T(1024)S(1)} %reduce_sum.48, f32[1024]{0:T(1024)S(1)} %multiply_reduce_fusion.1, f32[2048]{0:T(1024)S(1)} %multiply_reduce_fusion, f32[2048]{0:T(1024)S(1)} %bitcast.7, ...), kind=kOutput, calls=%fused_computation.10 | convolution fusion | flops 285278208 | bytes 9216000 | tf_op jit(solution)/shard_map/dot_general | solution.py:47
  97.2 0.0 reduce-scatter.2.cloned.1.call-update
  97.3 21.5 %reduce-scatter.2.cloned.1.call-done = f32[256,64]{0,1:T(8,128)} async-done(((f32[1024,64]{0,1:T(8,128)}), f32[256,64]{0,1:T(8,128)}) %reduce-scatter.2.cloned.1.call-update) | async-done | bytes 65552 | tf_op jit(solution)/shard_map/reduce_scatter | solution.py:56
  118.7 1.5 %broadcast_multiply_fusion = f32[256,64]{0,1:T(8,128)} fusion(f32[256,64]{0,1:T(8,128)} %reduce-scatter.2.cloned.1.call-done), kind=kLoop, calls=%fused_computation.12 | loop fusion | flops 16384 | bytes 131072 | tf_op jit(solution)/shard_map/mul | solution.py:57
  (7 shorter events, 0.1 us)
Async XLA Ops:
  6.5 47.9 %all-gather.5.cloned.1.call-start = ((), (), s32[]{:S(2)}) async-start(), calls=%async_computation.1 | async-start | bytes 1179648 | tf_op jit(solution)/shard_map/all_gather | solution.py:25
  7.3 111.5 %reduce-scatter.2.cloned.1.call-start = ((), (), s32[]{:S(2)}) async-start(), calls=%async_computation.2 | async-start | bytes 327680 | tf_op jit(solution)/shard_map/reduce_scatter | solution.py:56
  86.5 6.9 %copy-start = (f32[2048,1024]{1,0:T(8,128)S(1)}, f32[2048,1024]{1,0:T(8,128)}, u32[]{:S(2)}) copy-start(f32[2048,1024]{1,0:T(8,128)} %get-tuple-element.7) | copy-start | bytes 25165828
Sparse Core Ops, SparseCore 0:
  9.0 24.7 all-gather.4
  97.4 21.3 reduce-scatter.1
